TPU v7x, 128 devices: a whole 4x4x4 slice. The times are simulated.
128 devices in a mesh: row: 8 (over x, y_hi), col: 16 (over z, y_lo, core).
Axes of the slice: x: 4, y: 4 (y_hi: 2, y_lo: 2; y = y_hi * 2 + y_lo), z: 4, core: 2. Of those that a mesh axis runs over, the one named last changes fastest.
Arguments:
- normal_slab: float32 [8192, 16384], P('row', 'col'), may hold values from -6 to 6
- left_design: float32 [3, 1024, 8192], P(None, 'col', 'row'), may hold values from -1.2 to 1.2
- right_design: float32 [3, 1024, 16384], P(None, 'row', 'col'), may hold values from -1.2 to 1.2
- estimate: float32 [16384], P('col'), may hold values from -0.25 to 0.25
- observed: float32 [3, 1024], P(None, 'row'), may hold values from -6 to 6
- arc_id: int32 [3, 1024], P(None, 'row'), may hold values from 0 to 63
- arc_bias: float32 [64], replicated, may hold values from -5 to 5
Outputs:
- updated_slab: float32 [8192, 16384], P('row', 'col')
All inputs are finite; a program needn't handle non-finite values.
Results may differ from a plain program's by a relative error of at most 0.0001.
Values sent between devices are 32-bit elements; how exact they have to be, the bound alone decides.
A program may use at most 128 MiB of HBM per device.

v0:
```python
import jax
import jax.numpy as jnp
from jax import lax
from jax.sharding import PartitionSpec as P


def gathered_total(x, axis):
    tiles = lax.all_gather(x, axis)
    return tiles.sum(axis=0)


def contract(left_rows, right_rows, weights):
    return lax.dot_general(
        left_rows * weights[:, None],
        right_rows,
        (((0,), (0,)), ((), ())),
        precision=lax.Precision.HIGHEST,
    )


def local(normal_slab, left_design, right_design, estimate, observed, arc_id, arc_bias):
    highest = lax.Precision.HIGHEST
    one_hot = arc_id[:, :, None] == jnp.arange(arc_bias.shape[0], dtype=jnp.int32)[None, None, :]
    arc_offset = jnp.sum(jnp.where(one_hot, arc_bias[None, None, :], jnp.float32(0.0)), axis=2)
    running = normal_slab
    for number in range(right_design.shape[0]):
        partial_sum = jnp.dot(right_design[number], estimate, precision=highest)
        summed = gathered_total(partial_sum, "col")
        residual = observed[number] - summed - arc_offset[number]
        weights = 1.0 / (1.0 + residual * residual)
        left_all = lax.all_gather(left_design[number], "col", axis=0, tiled=True)
        right_rows = lax.all_gather(right_design[number], "row", axis=0, tiled=True)
        weight_rows = lax.all_gather(weights, "row", axis=0, tiled=True)
        running = running + contract(left_all, right_rows, weight_rows)
    return running


def solution(mesh):
    in_specs = (
        P("row", "col"),
        P(None, "col", "row"),
        P(None, "row", "col"),
        P("col"),
        P(None, "row"),
        P(None, "row"),
        P(),
    )
    out_specs = P("row", "col")
    return jax.shard_map(local, mesh=mesh, in_specs=in_specs, out_specs=out_specs, check_vma=False)
```

profile of v0, /device:TPU:1, one launch (start us, length us, event | category | flops | bytes accessed | tf_op | source)
XLA Modules:
  0.0 382.7 jit_solution(7969491137729842434)
XLA Ops:
  6.6 0.0 all-gather.32.cloned.1.call-start
  6.6 2.7 fusion.23
  9.3 0.0 all-gather.32.cloned.1.call-update
  9.4 0.0 all-gather.30.cloned.1.call-start
  9.4 0.9 fusion.24
  10.4 0.0 all-gather.30.cloned.1.call-update
  10.4 0.0 all-gather.28.cloned.1.call-start
  10.4 0.7 all-gather.28.cloned.1.call-update
  11.1 0.0 all-gather.26.cloned.1.call-start
  11.2 0.5 all-gather.26.cloned.1.call-update
  11.7 0.0 all-gather.24.cloned.1.call-start
  11.7 0.5 all-gather.24.cloned.1.call-update
  12.3 0.0 all-gather.22.cloned.1.call-start
  12.3 0.5 all-gather.22.cloned.1.call-update
  12.9 0.5 convolution_bitcast_fusion.2
  13.4 22.2 %all-gather.9 = f32[16,1,128]{2,1,0:T(1,128)S(1)} all-gather(f32[1,1,128]{2,1,0:T(1,128)S(1)} %convolution_bitcast_fusion.2), channel_id=3, replica_groups=mesh['row'=8,'col'=16] {'col'}, dimensions={0}, use_global_device_ids=true | all-gather | bytes 8704 | tf_op jit(solution)/shard_map/all_gather | solution.py:8
  35.6 0.5 convolution_bitcast_fusion.1
  36.1 16.1 %all-gather.11 = f32[16,1,128]{2,1,0:T(1,128)S(1)} all-gather(f32[1,1,128]{2,1,0:T(1,128)S(1)} %convolution_bitcast_fusion.1), channel_id=6, replica_groups=mesh['row'=8,'col'=16] {'col'}, dimensions={0}, use_global_device_ids=true | all-gather | bytes 8704 | tf_op jit(solution)/shard_map/all_gather | solution.py:8
  52.3 0.5 convolution_bitcast_fusion
  52.8 17.6 %all-gather.13 = f32[16,1,128]{2,1,0:T(1,128)S(1)} all-gather(f32[1,1,128]{2,1,0:T(1,128)S(1)} %convolution_bitcast_fusion), channel_id=9, replica_groups=mesh['row'=8,'col'=16] {'col'}, dimensions={0}, use_global_device_ids=true | all-gather | bytes 8704 | tf_op jit(solution)/shard_map/all_gather | solution.py:8
  70.4 0.1 select_reduce_fusion
  70.5 19.3 %all-gather.14 = f32[8,1,128]{2,1,0:T(1,128)S(1)} all-gather(f32[1,1,128]{2,1,0:T(1,128)S(1)} %get-tuple-element.12), channel_id=1, replica_groups=mesh['row'=8,'col'=16] {'row'}, dimensions={0}, use_global_device_ids=true | all-gather | bytes 4608 | tf_op jit(solution)/shard_map/all_gather | solution.py:33
  89.8 14.5 %all-gather.12 = f32[8,1,128]{2,1,0:T(1,128)S(1)} all-gather(f32[1,1,128]{2,1,0:T(1,128)S(1)} %get-tuple-element.13), channel_id=1, replica_groups=mesh['row'=8,'col'=16] {'row'}, dimensions={0}, use_global_device_ids=true | all-gather | bytes 4608 | tf_op jit(solution)/shard_map/all_gather | solution.py:33
  104.3 17.5 %all-gather.10 = f32[8,1,128]{2,1,0:T(1,128)S(1)} all-gather(f32[1,1,128]{2,1,0:T(1,128)S(1)} %get-tuple-element.11), channel_id=1, replica_groups=mesh['row'=8,'col'=16] {'row'}, dimensions={0}, use_global_device_ids=true | all-gather | bytes 4608 | tf_op jit(solution)/shard_map/all_gather | solution.py:33
  121.9 0.3 all-gather.30.cloned.1.call-done
  122.2 18.2 %fusion = f32[1024,1024]{1,0:T(8,128)} fusion(f32[1,1024,1024]{2,1,0:T(8,128)} %all-gather.32.cloned.1.call-done, f32[1,1024,1024]{2,1,0:T(8,128)} %all-gather.30.cloned.1.call-done, f32[1024]{0:T(1024)S(1)} %bitcast.105), kind=kOutput, calls=%fused_computation | convolution fusion | flops 12885950464 | bytes 12587008 | tf_op jit(solution)/shard_map/dot_general | solution.py:13
  140.4 54.8 %all-gather.28.cloned.1.call-done = f32[1,1024,1024]{2,1,0:T(8,128)} async-done(((f32[1,128,1024]{2,1,0:T(8,128)}), f32[1,1024,1024]{2,1,0:T(8,128)}) %all-gather.28.cloned.1.call-update) | async-done | bytes 4194320 | tf_op jit(solution)/shard_map/all_gather | solution.py:32
  195.2 37.8 %all-gather.26.cloned.1.call-done = f32[1,1024,1024]{2,1,0:T(8,128)} async-done(((f32[1,64,1024]{2,1,0:T(8,128)}), f32[1,1024,1024]{2,1,0:T(8,128)}) %all-gather.26.cloned.1.call-update) | async-done | bytes 4194320 | tf_op jit(solution)/shard_map/all_gather | solution.py:31
  232.9 18.3 %fusion.2 = f32[1024,1024]{1,0:T(8,128)} fusion(f32[1,1024,1024]{2,1,0:T(8,128)} %all-gather.28.cloned.1.call-done, f32[1,1024,1024]{2,1,0:T(8,128)} %all-gather.26.cloned.1.call-done, f32[1024]{0:T(1024)S(1)} %bitcast.104), kind=kOutput, calls=%fused_computation.3 | convolution fusion | flops 12885950464 | bytes 12587008 | tf_op jit(solution)/shard_map/dot_general | solution.py:13
  251.2 54.6 %all-gather.24.cloned.1.call-done = f32[1,1024,1024]{2,1,0:T(8,128)} async-done(((f32[1,128,1024]{2,1,0:T(8,128)}), f32[1,1024,1024]{2,1,0:T(8,128)}) %all-gather.24.cloned.1.call-update) | async-done | bytes 4194320 | tf_op jit(solution)/shard_map/all_gather | solution.py:32
  305.8 37.8 %all-gather.22.cloned.1.call-done = f32[1,1024,1024]{2,1,0:T(8,128)} async-done(((f32[1,64,1024]{2,1,0:T(8,128)}), f32[1,1024,1024]{2,1,0:T(8,128)}) %all-gather.22.cloned.1.call-update) | async-done | bytes 4194320 | tf_op jit(solution)/shard_map/all_gather | solution.py:31
  343.6 32.2 %add_add_fusion = f32[1024,1024]{1,0:T(8,128)} fusion(f32[1024,1024]{1,0:T(8,128)} %fusion, f32[1024,1024]{1,0:T(8,128)} %fusion.2, f32[1024,1024]{1,0:T(8,128)} %param.7, f32[1,1024,1024]{2,1,0:T(8,128)} %all-gather.24.cloned.1.call-done, f32[1,1024,1024]{2,1,0:T(8,128)} %all-gather.22.cloned.1.call-done, f32[1024]{0:T(1024)S(1)} %bitcast.103), kind=kOutput, calls=%fused_computation.9 | convolution fusion | flops 12889096192 | bytes 25169920 | tf_op jit(solution)/shard_map/dot_general | solution.py:13
  (17 shorter events, 0.1 us)
Async XLA Ops:
  6.5 6.3 %copy-start = (f32[1024]{0:T(1024)S(1)}, f32[1024]{0:T(1024)}, u32[]{:S(2)}) copy-start(f32[1024]{0:T(1024)} %param.10) | copy-start | bytes 12292
  6.5 6.3 %copy-start.1 = (f32[3,128,1024]{2,1,0:T(8,128)S(1)}, f32[3,128,1024]{2,1,0:T(8,128)}, u32[]{:S(2)}) copy-start(f32[3,128,1024]{2,1,0:T(8,128)} %param.9) | copy-start | bytes 4718596
  6.5 2.9 copy-start.2
  6.5 63.8 %copy-start.3 = (s32[3,128]{1,0:T(4,128)S(1)}, s32[3,128]{1,0:T(4,128)}, u32[]{:S(2)}) copy-start(s32[3,128]{1,0:T(4,128)} %param.12) | copy-start | bytes 4612
  6.5 63.8 %copy-start.5 = (f32[64]{0:T(128)S(1)}, f32[64]{0:T(128)}, u32[]{:S(2)}) copy-start(f32[64]{0:T(128)} %param.13) | copy-start | bytes 772
  6.5 63.9 %copy-start.4 = (f32[3,128]{1,0:T(4,128)S(1)}, f32[3,128]{1,0:T(4,128)}, u32[]{:S(2)}) copy-start(f32[3,128]{1,0:T(4,128)} %param.11) | copy-start | bytes 4612
  6.6 115.3 %all-gather.32.cloned.1.call-start = ((), (), s32[]{:S(2)}) async-start(), calls=%async_computation.5 | async-start | bytes 4718592 | tf_op jit(solution)/shard_map/all_gather | solution.py:32
  9.4 112.8 %all-gather.30.cloned.1.call-start = ((), (), s32[]{:S(2)}) async-start(), calls=%async_computation.4 | async-start | bytes 4456448 | tf_op jit(solution)/shard_map/all_gather | solution.py:31
  10.4 184.8 %all-gather.28.cloned.1.call-start = ((), (), s32[]{:S(2)}) async-start(), calls=%async_computation.3 | async-start | bytes 4718592 | tf_op jit(solution)/shard_map/all_gather | solution.py:32
  11.1 221.8 %all-gather.26.cloned.1.call-start = ((), (), s32[]{:S(2)}) async-start(), calls=%async_computation.2 | async-start | bytes 4456448 | tf_op jit(solution)/shard_map/all_gather | solution.py:31
  11.7 294.1 %all-gather.24.cloned.1.call-start = ((), (), s32[]{:S(2)}) async-start(), calls=%async_computation.1 | async-start | bytes 4718592 | tf_op jit(solution)/shard_map/all_gather | solution.py:32
  12.3 331.3 %all-gather.22.cloned.1.call-start = ((), (), s32[]{:S(2)}) async-start(), calls=%async_computation | async-start | bytes 4456448 | tf_op jit(solution)/shard_map/all_gather | solution.py:31
Sparse Core Ops, SparseCore 0:
  9.7 74.3 all-gather.31
  85.9 36.2 all-gather.29
  124.5 70.5 all-gather.27
  196.7 36.1 all-gather.25
  235.1 70.6 all-gather.23
  307.4 36.1 all-gather.21
where the time goes:
time: 383 us
  waiting for transfers between devices  188 us (49%)
  blocking collectives  107 us (28%)
  matrix products  70.3 us (18%)
  between operations  13.5 us (4%)
    all_gather x3, waiting for transfers between devices, local(): right_rows = lax.all_gather(right_design[number], 'row', axis=0, tiled=True)  109 us
    all_gather x3, waiting for transfers between devices, local(): left_all = lax.all_gather(left_design[number], 'col', axis=0, tiled=True)  75.9 us
    dot_general x3, matrix products, contract(): lax.dot_general(left_rows * weights[:, None], right_rows, (((0,), (0,)),...  68.7 us
    all_gather x3, blocking collectives, gathered_total(): tiles = lax.all_gather(x, axis)  55.8 us
    all_gather x3, blocking collectives, local(): weight_rows = lax.all_gather(weights, 'row', axis=0, tiled=True)  51.4 us
  transfers between devices with their start and end apart: 6, of which 5 were waited for; matrix products, arithmetic and copies ran while one was open for 10% of the time, Pallas kernels for 0%

commit v1 on v0

--- a/solution.py
+++ b/solution.py
@@ -28,7 +28,10 @@
         summed = gathered_total(partial_sum, "col")
         residual = observed[number] - summed - arc_offset[number]
         weights = 1.0 / (1.0 + residual * residual)
-        left_all = lax.all_gather(left_design[number], "col", axis=0, tiled=True)
+        left_all = jnp.concatenate(
+            lax.all_to_all(jnp.stack([left_design[number]] * lax.axis_size("col")), "col", 0, 0),
+            axis=0,
+        )
         right_rows = lax.all_gather(right_design[number], "row", axis=0, tiled=True)
         weight_rows = lax.all_gather(weights, "row", axis=0, tiled=True)
         running = running + contract(left_all, right_rows, weight_rows)

time: 383 us -> 423 us (1.10)
  the two profiles are of different devices: /device:TPU:1 before, /device:TPU:0 now
where the time goes in v1:
time: 423 us; the launch traced here: 422 us
  blocking collectives  249 us (59%)
  matrix products  68.5 us (16%)
  waiting for transfers between devices  60.3 us (14%)
  other arithmetic  13.7 us (3%)
  between operations  13.2 us (3%)
  starting transfers between devices  9.32 us (2%)
  local copies, waits for them, and re-layouts  8.33 us (2%)
    all_gather x3, blocking collectives, gathered_total(): tiles = lax.all_gather(x, axis)  106 us
    all_to_all x1, blocking collectives, local(): lax.all_to_all(jnp.stack([left_design[number]] * lax.axis_size('col')), '...  79.7 us
    dot_general x3, matrix products, contract(): lax.dot_general(left_rows * weights[:, None], right_rows, (((0,), (0,)),...  67 us
    all_gather x3, blocking collectives, local(): weight_rows = lax.all_gather(weights, 'row', axis=0, tiled=True)  62.7 us
    all_to_all x2, waiting for transfers between devices, local(): lax.all_to_all(jnp.stack([left_design[number]] * lax.axis_size('col')), '...  58.9 us
    mul x3, other arithmetic, contract(): left_rows * weights[:, None]  13.5 us
    all_to_all x2, starting transfers between devices, local(): lax.all_to_all(jnp.stack([left_design[number]] * lax.axis_size('col')), '...  9.24 us
  transfers between devices with their start and end apart: 5, of which 1 were waited for; matrix products, arithmetic and copies ran while one was open for 13% of the time, Pallas kernels for 0%

profile of v1, /device:TPU:0, one launch (start us, length us, event | category | flops | bytes accessed | tf_op | source)
XLA Modules:
  0.0 422.1 jit_solution(4852006620274418061)
XLA Ops:
  6.5 0.0 all-gather.20.cloned.1.call-start
  6.5 2.7 fusion.20
  9.2 0.0 all-gather.20.cloned.1.call-update
  9.3 0.0 all-gather.18.cloned.1.call-start
  9.3 0.7 all-gather.18.cloned.1.call-update
  10.0 0.1 slice_bitcast_fusion.2
  10.1 0.5 stack.11
  10.6 79.7 %all_to_all.15 = f32[16,64,1024]{2,1,0:T(8,128)} all-to-all(f32[16,64,1024]{2,1,0:T(8,128)S(1)} %stack.11), channel_id=1, replica_groups=mesh['row'=8,'col'=16] {'col'}, dimensions={0} | all-to-all | bytes 8388608 | tf_op jit(solution)/shard_map/all_to_all | solution.py:32
  90.3 2.5 stack.10
  92.9 4.6 %all-to-all-start.1 = ((f32[16,64,1024]{2,1,0:T(8,128)}), f32[16,64,1024]{2,1,0:T(8,128)}, u32[]{:S(2)}, u32[]{:S(2)}) async-start(f32[16,64,1024]{2,1,0:T(8,128)} %stack.10), calls=%async_computation.1 | async-start | bytes 8388608 | tf_op jit(solution)/shard_map/all_to_all | solution.py:32
  97.4 0.0 all-gather.16.cloned.1.call-start
  97.5 0.7 all-gather.16.cloned.1.call-update
  98.2 58.9 %all-to-all-done.1 = f32[16,64,1024]{2,1,0:T(8,128)} async-done(((f32[16,64,1024]{2,1,0:T(8,128)}), f32[16,64,1024]{2,1,0:T(8,128)}, u32[]{:S(2)}, u32[]{:S(2)}) %all-to-all-start.1) | async-done | bytes 4194336 | tf_op jit(solution)/shard_map/all_to_all | solution.py:32
  157.1 2.5 stack.9
  159.6 4.7 %all-to-all-start = ((f32[16,64,1024]{2,1,0:T(8,128)}), f32[16,64,1024]{2,1,0:T(8,128)}, u32[]{:S(2)}, u32[]{:S(2)}) async-start(f32[16,64,1024]{2,1,0:T(8,128)} %stack.9), calls=%async_computation | async-start | bytes 8388608 | tf_op jit(solution)/shard_map/all_to_all | solution.py:32
  164.3 0.5 convolution_bitcast_fusion.2
  164.8 72.6 %all-gather.6 = f32[16,1,128]{2,1,0:T(1,128)S(1)} all-gather(f32[1,1,128]{2,1,0:T(1,128)S(1)} %convolution_bitcast_fusion.2), channel_id=2, replica_groups=mesh['row'=8,'col'=16] {'col'}, dimensions={0}, use_global_device_ids=true | all-gather | bytes 8704 | tf_op jit(solution)/shard_map/all_gather | solution.py:8
  237.5 0.5 convolution_bitcast_fusion.1
  238.0 17.4 %all-gather.8 = f32[16,1,128]{2,1,0:T(1,128)S(1)} all-gather(f32[1,1,128]{2,1,0:T(1,128)S(1)} %convolution_bitcast_fusion.1), channel_id=4, replica_groups=mesh['row'=8,'col'=16] {'col'}, dimensions={0}, use_global_device_ids=true | all-gather | bytes 8704 | tf_op jit(solution)/shard_map/all_gather | solution.py:8
  255.4 0.5 convolution_bitcast_fusion
  255.9 16.3 %all-gather.10 = f32[16,1,128]{2,1,0:T(1,128)S(1)} all-gather(f32[1,1,128]{2,1,0:T(1,128)S(1)} %convolution_bitcast_fusion), channel_id=6, replica_groups=mesh['row'=8,'col'=16] {'col'}, dimensions={0}, use_global_device_ids=true | all-gather | bytes 8704 | tf_op jit(solution)/shard_map/all_gather | solution.py:8
  272.3 0.1 select_reduce_fusion
  272.4 23.2 %all-gather.11 = f32[8,1,128]{2,1,0:T(1,128)S(1)} all-gather(f32[1,1,128]{2,1,0:T(1,128)S(1)} %get-tuple-element.12), channel_id=1, replica_groups=mesh['row'=8,'col'=16] {'row'}, dimensions={0}, use_global_device_ids=true | all-gather | bytes 4608 | tf_op jit(solution)/shard_map/all_gather | solution.py:36
  295.6 18.0 %all-gather.9 = f32[8,1,128]{2,1,0:T(1,128)S(1)} all-gather(f32[1,1,128]{2,1,0:T(1,128)S(1)} %get-tuple-element.13), channel_id=1, replica_groups=mesh['row'=8,'col'=16] {'row'}, dimensions={0}, use_global_device_ids=true | all-gather | bytes 4608 | tf_op jit(solution)/shard_map/all_gather | solution.py:36
  313.6 21.5 %all-gather.7 = f32[8,1,128]{2,1,0:T(1,128)S(1)} all-gather(f32[1,1,128]{2,1,0:T(1,128)S(1)} %get-tuple-element.11), channel_id=1, replica_groups=mesh['row'=8,'col'=16] {'row'}, dimensions={0}, use_global_device_ids=true | all-gather | bytes 4608 | tf_op jit(solution)/shard_map/all_gather | solution.py:36
  335.1 4.5 %bitcast_multiply_fusion = f32[1024,1024]{1,0:T(8,128)} fusion(f32[16,64,1024]{2,1,0:T(8,128)} %all_to_all.15, f32[1024]{0:T(1024)S(1)} %bitcast.109), kind=kLoop, calls=%fused_computation.2 | loop fusion | flops 1048576 | bytes 8392704 | tf_op jit(solution)/shard_map/mul | solution.py:14
  339.6 4.5 %bitcast_multiply_fusion.1 = f32[1024,1024]{1,0:T(8,128)} fusion(f32[16,64,1024]{2,1,0:T(8,128)} %all-to-all-done.1, f32[1024]{0:T(1024)S(1)} %bitcast.108), kind=kLoop, calls=%fused_computation.5 | loop fusion | flops 1048576 | bytes 8392704 | tf_op jit(solution)/shard_map/mul | solution.py:14
  344.1 0.0 all-to-all-done
  344.1 4.5 %bitcast_multiply_fusion.2 = f32[1024,1024]{1,0:T(8,128)} fusion(f32[16,64,1024]{2,1,0:T(8,128)} %all-to-all-done, f32[1024]{0:T(1024)S(1)} %bitcast.107), kind=kLoop, calls=%fused_computation.8 | loop fusion | flops 1048576 | bytes 8392704 | tf_op jit(solution)/shard_map/mul | solution.py:14
  348.6 17.6 %fusion = f32[1024,1024]{1,0:T(8,128)} fusion(f32[1024,1024]{1,0:T(8,128)} %bitcast_multiply_fusion, f32[1,1024,1024]{2,1,0:T(8,128)} %all-gather.20.cloned.1.call-done), kind=kOutput, calls=%fused_computation | convolution fusion | flops 12884901888 | bytes 12582912 | tf_op jit(solution)/shard_map/dot_general | solution.py:13
  366.2 17.6 %fusion.2 = f32[1024,1024]{1,0:T(8,128)} fusion(f32[1024,1024]{1,0:T(8,128)} %bitcast_multiply_fusion.1, f32[1,1024,1024]{2,1,0:T(8,128)} %all-gather.18.cloned.1.call-done), kind=kOutput, calls=%fused_computation.3 | convolution fusion | flops 12884901888 | bytes 12582912 | tf_op jit(solution)/shard_map/dot_general | solution.py:13
  383.7 31.8 %add_add_fusion = f32[1024,1024]{1,0:T(8,128)} fusion(f32[1024,1024]{1,0:T(8,128)} %fusion, f32[1024,1024]{1,0:T(8,128)} %fusion.2, f32[1024,1024]{1,0:T(8,128)} %param.7, f32[1024,1024]{1,0:T(8,128)} %bitcast_multiply_fusion.2, f32[1,1024,1024]{2,1,0:T(8,128)} %all-gather.16.cloned.1.call-done), kind=kOutput, calls=%fused_computation.9 | convolution fusion | flops 12888047616 | bytes 25165824 | tf_op jit(solution)/shard_map/dot_general | solution.py:13
  (21 shorter events, 0.1 us)
Async XLA Ops:
  6.5 157.8 %copy-start = (f32[1024]{0:T(1024)S(1)}, f32[1024]{0:T(1024)}, u32[]{:S(2)}) copy-start(f32[1024]{0:T(1024)} %param.10) | copy-start | bytes 12292
  6.5 3.5 copy-start.3
  6.5 342.0 %all-gather.20.cloned.1.call-start = ((), (), s32[]{:S(2)}) async-start(), calls=%async_computation.5 | async-start | bytes 4718592 | tf_op jit(solution)/shard_map/all_gather | solution.py:35
  9.3 356.9 %all-gather.18.cloned.1.call-start = ((), (), s32[]{:S(2)}) async-start(), calls=%async_computation.4 | async-start | bytes 4718592 | tf_op jit(solution)/shard_map/all_gather | solution.py:35
  92.9 64.2 %all-to-all-start.1 = ((f32[16,64,1024]{2,1,0:T(8,128)}), f32[16,64,1024]{2,1,0:T(8,128)}, u32[]{:S(2)}, u32[]{:S(2)}) async-start(f32[16,64,1024]{2,1,0:T(8,128)} %stack.10), calls=%async_computation.1 | async-start | bytes 8388608 | tf_op jit(solution)/shard_map/all_to_all | solution.py:32
  97.4 286.3 %all-gather.16.cloned.1.call-start = ((), (), s32[]{:S(2)}) async-start(), calls=%async_computation.3 | async-start | bytes 4718592 | tf_op jit(solution)/shard_map/all_gather | solution.py:35
  159.6 4.7 %copy-start.2 = (f32[3,128,1024]{2,1,0:T(8,128)S(1)}, f32[3,128,1024]{2,1,0:T(8,128)}, u32[]{:S(2)}) copy-start(f32[3,128,1024]{2,1,0:T(8,128)} %param.9) | copy-start | bytes 4718596
  159.6 112.7 %copy-start.4 = (s32[3,128]{1,0:T(4,128)S(1)}, s32[3,128]{1,0:T(4,128)}, u32[]{:S(2)}) copy-start(s32[3,128]{1,0:T(4,128)} %param.12) | copy-start | bytes 4612
  159.6 112.7 %copy-start.6 = (f32[64]{0:T(128)S(1)}, f32[64]{0:T(128)}, u32[]{:S(2)}) copy-start(f32[64]{0:T(128)} %param.13) | copy-start | bytes 772
  159.6 112.8 %copy-start.5 = (f32[3,128]{1,0:T(4,128)S(1)}, f32[3,128]{1,0:T(4,128)}, u32[]{:S(2)}) copy-start(f32[3,128]{1,0:T(4,128)} %param.11) | copy-start | bytes 4612
  159.6 184.5 %all-to-all-start = ((f32[16,64,1024]{2,1,0:T(8,128)}), f32[16,64,1024]{2,1,0:T(8,128)}, u32[]{:S(2)}, u32[]{:S(2)}) async-start(f32[16,64,1024]{2,1,0:T(8,128)} %stack.9), calls=%async_computation | async-start | bytes 8388608 | tf_op jit(solution)/shard_map/all_to_all | solution.py:32
  383.7 31.8 %copy-start.1 = (f32[1024]{0:T(1024)S(1)}, f32[1024]{0:T(1024)}, u32[]{:S(2)}) copy-start(f32[1024]{0:T(1024)} %param.10) | copy-start | bytes 12292
Sparse Core Ops, SparseCore 0:
  9.7 96.5 all-gather.19
  108.6 86.0 all-gather.17
  197.1 73.6 all-gather.15
